TPU v7x, 32 devices: a whole 2x2x4 slice. The times are simulated.
32 devices in a mesh: seq: 8 (over z, x), exp: 4 (over y, core).
Axes of the slice: x: 2, y: 2, z: 4, core: 2. Of those that a mesh axis runs over, the one named last changes fastest.
Arguments:
- residual: bfloat16 [4096, 8192], P('seq', 'exp'), may hold values from -16 to 16
- queries: bfloat16 [4096, 4096], P('seq', 'exp'), may hold values from -6 to 6
- keys: bfloat16 [4096, 4096], P('seq', 'exp'), may hold values from -10 to 10
- values: bfloat16 [4096, 4096], P('seq', 'exp'), may hold values from -6 to 6
- documents: int32 [4096], replicated, may hold values from 0 to 1, as said below
- out_proj: bfloat16 [4096, 8192], P(None, 'exp'), may hold values from -0.09375 to 0.09375
- modality: int32 [4096], P('seq'), may hold values from 0 to 1, as said below
- norm_gain: float32 [2, 8192], P(None, 'exp'), may hold values from 0.25 to 1.75
- picks: int32 [4, 64], replicated, may hold values from 0 to 4095, as said below
- router: bfloat16 [8192, 4], P(None, 'exp'), may hold values from -0.0625 to 0.0625
- w_gate: bfloat16 [4, 8192, 4096], P('exp', None, 'seq'), may hold values from -0.0625 to 0.0625
- w_up: bfloat16 [4, 8192, 4096], P('exp', None, 'seq'), may hold values from -0.0625 to 0.0625
- w_down: bfloat16 [4, 4096, 8192], P('exp', 'seq'), may hold values from -0.09375 to 0.09375
Outputs:
- layer_out: bfloat16 [4096, 8192], P('seq', 'exp')
Inputs may be any that keep to these rules, and one draw needn't show every extreme that they name: `modality`: 0 marks a text token, 1 an image token. `documents`: 0 for the first document, 1 for the second; the second begins between position 1024 and 3072. `picks`: row e lists 64 different positions in ascending order; all carry modality 0 for e < 2 and modality 1 otherwise. Within each aligned block of 512 positions (the tokens of one index of seq) a row lists at most 16 positions, and every row lists exactly 16 in some block.
All inputs are finite; a program needn't handle non-finite values.
Results may differ from a plain program's by a relative error of at most 0.0035.
Values may be sent and summed in bfloat16 or wider, within the bound.
A program may use at most 128 MiB of HBM per device.

v0:
```python
import math
import jax
import jax.numpy as jnp
from jax import lax
from jax.sharding import PartitionSpec as P

D = 8192
HD = 128
block_rows = 512


def shards(
    residual,
    queries,
    keys,
    values,
    documents,
    out_proj,
    modality,
    norm_gain,
    picks,
    router,
    w_gate,
    w_up,
    w_down,
):
    tokens = queries.shape[0]
    heads_here = queries.shape[1] // HD
    seq_pos = lax.axis_index("seq")
    start_row = seq_pos * tokens
    query_pos = start_row + jnp.arange(tokens, dtype=jnp.int32)
    query_doc = lax.dynamic_slice_in_dim(documents, start_row, tokens, 0)
    query_heads = queries.reshape(tokens, heads_here, HD)
    score_scale = 1.0 / math.sqrt(HD)

    def attend(state, key_rows, value_rows, key_start):
        row_count = key_rows.shape[0]
        key_pos = key_start + jnp.arange(row_count, dtype=jnp.int32)
        key_doc = lax.dynamic_slice_in_dim(documents, key_start, row_count, 0)
        scores = (
            jnp.einsum(
                "qhd,khd->qhk",
                query_heads,
                key_rows.reshape(row_count, heads_here, HD),
                preferred_element_type=jnp.float32,
            )
            * score_scale
        )
        allowed = (key_pos[None, :] <= query_pos[:, None]) & (
            key_doc[None, :] == query_doc[:, None]
        )
        scores = jnp.where(allowed[:, None, :], scores, -jnp.inf)
        running_max, running_sum, running_out = state
        new_max = jnp.maximum(running_max, jnp.max(scores, axis=2))
        factor = jnp.exp(running_max - new_max)
        weights = jnp.exp(scores - new_max[:, :, None])
        running_sum = running_sum * factor + jnp.sum(weights, axis=2)
        running_out = running_out * factor[:, :, None] + jnp.einsum(
            "qhk,khd->qhd",
            weights.astype(jnp.bfloat16),
            value_rows.reshape(row_count, heads_here, HD),
            preferred_element_type=jnp.float32,
        )
        return (new_max, running_sum, running_out)

    def visit_block(state, key_rows, value_rows, key_start):
        row_count = key_rows.shape[0]
        last_doc = lax.dynamic_index_in_dim(documents, key_start + row_count - 1, 0, keepdims=False)
        beyond = (key_start > query_pos[tokens - 1]) | (last_doc < query_doc[0])
        return lax.cond(
            beyond,
            lambda inner_state: inner_state,
            lambda inner_state: attend(inner_state, key_rows, value_rows, key_start),
            state,
        )

    initial = (
        jnp.full((tokens, heads_here), -1e30, jnp.float32),
        jnp.zeros((tokens, heads_here), jnp.float32),
        jnp.zeros((tokens, heads_here, HD), jnp.float32),
    )
    state = initial
    key_piece = lax.all_gather(keys, "seq", axis=0, tiled=True)
    value_piece = lax.all_gather(values, "seq", axis=0, tiled=True)
    row_count = key_piece.shape[0]
    blocks = row_count // block_rows
    key_stack = key_piece.reshape(blocks, block_rows, key_piece.shape[1])
    value_stack = value_piece.reshape(blocks, block_rows, value_piece.shape[1])

    def scan_step(inner_state, block_item):
        block_index, key_rows, value_rows = block_item
        return (visit_block(inner_state, key_rows, value_rows, block_index * block_rows), None)

    state, unused = lax.scan(
        scan_step, state, (jnp.arange(blocks, dtype=jnp.int32), key_stack, value_stack)
    )
    running_max, running_sum, running_out = state
    attended = (
        (running_out / running_sum[:, :, None])
        .reshape(tokens, heads_here * HD)
        .astype(jnp.bfloat16)
    )
    mixed = jnp.dot(
        lax.all_gather(attended, "exp", axis=1, tiled=True),
        out_proj,
        preferred_element_type=jnp.float32,
    )
    hidden_state = (residual.astype(jnp.float32) + mixed).astype(jnp.bfloat16)
    hidden_wide = hidden_state.astype(jnp.float32)
    square_total = lax.psum(jnp.sum(hidden_wide * hidden_wide, axis=1), "exp")
    inverse = lax.rsqrt(square_total / D + 1e-05)
    gain_rows = jnp.where(modality[:, None] == 0, norm_gain[0][None, :], norm_gain[1][None, :])
    normed = (hidden_wide * inverse[:, None] * gain_rows).astype(jnp.bfloat16)
    capacity = tokens // 32
    inside = (picks >= start_row) & (picks < start_row + tokens)
    slot_index = jnp.cumsum(inside.astype(jnp.int32), axis=1) - 1
    matched = inside[:, None, :] & (
        slot_index[:, None, :] == jnp.arange(capacity, dtype=jnp.int32)[None, :, None]
    )
    local_index = jnp.sum(jnp.where(matched, picks[:, None, :] - start_row, 0), axis=2)
    filled = jnp.any(matched, axis=2)
    rows_out = jnp.take(normed, local_index.T, axis=0)
    rows_out = jnp.where(filled.T[:, :, None], rows_out, jnp.zeros_like(rows_out))
    arrived = lax.all_to_all(rows_out, "exp", split_axis=1, concat_axis=1, tiled=True)
    expert_rows = arrived.reshape(capacity, D)
    logits = jnp.dot(expert_rows, router, preferred_element_type=jnp.float32)[:, 0]
    piece = lax.all_gather(expert_rows, "seq", axis=0, tiled=True)
    gate_part = jnp.dot(piece, w_gate[0], preferred_element_type=jnp.float32)
    up_part = jnp.dot(piece, w_up[0], preferred_element_type=jnp.float32)
    inner_act = (jax.nn.silu(gate_part) * up_part).astype(jnp.bfloat16)
    summed = lax.psum_scatter(
        jnp.dot(inner_act, w_down[0], preferred_element_type=jnp.float32).astype(jnp.bfloat16),
        "seq",
        scatter_dimension=0,
        tiled=True,
    ).astype(jnp.float32)
    weighted = (jax.nn.sigmoid(logits)[:, None] * summed).astype(jnp.bfloat16)
    own_expert = lax.axis_index("exp")
    own_index = lax.dynamic_index_in_dim(local_index, own_expert, 0, keepdims=False)
    own_filled = lax.dynamic_index_in_dim(filled, own_expert, 0, keepdims=False)
    placing = (
        (jnp.arange(tokens, dtype=jnp.int32)[:, None] == own_index[None, :]) & own_filled[None, :]
    ).astype(jnp.bfloat16)
    spread = jnp.dot(placing, weighted, preferred_element_type=jnp.float32)
    expert_add = lax.psum_scatter(
        spread.astype(jnp.bfloat16), "exp", scatter_dimension=1, tiled=True
    ).astype(jnp.float32)
    return (hidden_wide + expert_add).astype(jnp.bfloat16)


def solution(mesh):
    return jax.shard_map(
        shards,
        mesh=mesh,
        in_specs=(
            P("seq", "exp"),
            P("seq", "exp"),
            P("seq", "exp"),
            P("seq", "exp"),
            P(),
            P(None, "exp"),
            P("seq"),
            P(None, "exp"),
            P(),
            P(None, "exp"),
            P("exp", None, "seq"),
            P("exp", None, "seq"),
            P("exp", "seq", None),
        ),
        out_specs=P("seq", "exp"),
        check_vma=False,
    )
```

profile of v0, /device:TPU:0, one launch (start us, length us, event | category | flops | bytes accessed | tf_op | source)
XLA Modules:
  0.0 667.6 jit_solution(14505423510101249050)
XLA Ops:
  11.0 125.7 %all-gather.5.cloned.1.call-done = bf16[4096,1024]{1,0:T(8,128)(2,1)} async-done(((bf16[512,1024]{1,0:T(8,128)(2,1)}), bf16[4096,1024]{1,0:T(8,128)(2,1)}) %all-gather.5.cloned.1.call-update) | async-done | bytes 8388624 | tf_op jit(solution)/shard_map/all_gather | solution.py:83
  136.7 11.6 %copy.57 = bf16[8,512,1024]{1,2,0:T(8,128)(2,1)} copy(bf16[8,512,1024]{2,1,0:T(8,128)(2,1)} %bitcast.77) | data formatting | bytes 16777216 | tf_op jit(solution)/shard_map/while | solution.py:94
  148.3 113.2 %all-gather.7.cloned.1.call-done = bf16[4096,1024]{1,0:T(8,128)(2,1)} async-done(((bf16[512,1024]{1,0:T(8,128)(2,1)}), bf16[4096,1024]{1,0:T(8,128)(2,1)}) %all-gather.7.cloned.1.call-update) | async-done | bytes 8388624 | tf_op jit(solution)/shard_map/all_gather | solution.py:84
  261.5 11.4 %copy.59 = bf16[8,512,1024]{1,2,0:T(8,128)(2,1)} copy(bf16[8,512,1024]{2,1,0:T(8,128)(2,1)} %bitcast.78) | data formatting | bytes 16777216 | tf_op jit(solution)/shard_map/while | solution.py:94
  273.1 55.4 %while.18 = (s32[]{:T(128)}, f32[512,8]{0,1:T(8,128)S(1)}, f32[512,8]{0,1:T(8,128)S(1)}, f32[512,8,128]{2,0,1:T(8,128)S(1)}, s32[8]{0:T(128)S(1)}, /*index=5*/s3...) while((s32[]{:T(128)}, f32[512,8]{0,1:T(8,128)S(1)}, ...), condition=%wide.region_5.6_spmd, body=%wide.region_0.5_spmd.sunk | while | flops 1098654208 | bytes 38025672 | solution.py:94
  278.7 9.6 %conditional.2 = (f32[512,8]{0,1:T(8,128)S(1)}, f32[512,8]{0,1:T(8,128)S(1)}, f32[512,8,128]{2,0,1:T(8,128)S(1)}) conditional(s32[]{:T(128)} %convert_element_type.103, (s32[]{:T(128)}, s32[512]{0:T(512)S(1)}, s32[4096]{0:T(1024)}, s32[512]{0:T(512)S(1)}, bf16[8,512,1024]{1,2,0:T(8,128)(2,1)}, /*index=5*/s32[]{:T(128)}, ...), branch_computations={%region_1.3_spmd, %region_4.4_spmd} | conditional | flops 1098654208 | bytes 37992520 | solution.py:70
  279.8 1.7 constant_dynamic-slice_fusion
  283.2 1.7 fusion.1
  285.0 3.4 bitcast_add_fusion
  328.5 1.8 copy.60
  330.3 2.8 divide_convert_fusion
  334.3 79.5 %all-gather.9.cloned.1.call-done = bf16[512,4096]{0,1:T(8,128)(2,1)} async-done(((bf16[512,1024]{0,1:T(8,128)(2,1)}), bf16[512,4096]{0,1:T(8,128)(2,1)}) %all-gather.9.cloned.1.call-update) | async-done | bytes 4194320 | tf_op jit(solution)/shard_map/all_gather | solution.py:104
  413.8 14.2 %fusion.18 = (f32[512]{0:T(512)S(1)}, bf16[512,2048]{1,0:T(8,128)(2,1)S(1)}) fusion(bf16[512,4096]{0,1:T(8,128)(2,1)} %all-gather.9.cloned.1.call-done, bf16[4096,2048]{1,0:T(8,128)(2,1)} %param.22, bf16[512,2048]{1,0:T(8,128)(2,1)} %param.17), kind=kOutput, calls=%fused_computation.30 | convolution fusion | flops 8596226048 | bytes 25167872 | tf_op jit(solution)/shard_map/dot_general | solution.py:103
  428.0 5.9 psum.7
  433.9 2.1 fusion.20
  436.0 2.8 gather_fusion
  439.3 8.7 %all_to_all.5 = bf16[16,4,2048]{2,0,1:T(8,128)(2,1)S(1)} all-to-all(bf16[16,4,2048]{2,0,1:T(8,128)(2,1)S(1)} %fusion.34), channel_id=1, replica_groups=mesh['seq'=8,'exp'=4] {'exp'}, dimensions={1} | all-to-all | bytes 524288 | tf_op jit(solution)/shard_map/all_to_all | solution.py:124
  448.8 49.2 %all-gather.11.cloned.1.call-done = bf16[128,8192]{1,0:T(8,128)(2,1)} async-done(((bf16[16,8192]{1,0:T(8,128)(2,1)}), bf16[128,8192]{1,0:T(8,128)(2,1)}) %all-gather.11.cloned.1.call-update) | async-done | bytes 2097168 | tf_op jit(solution)/shard_map/all_gather | solution.py:127
  498.0 5.4 fusion.16
  503.5 9.6 %convolution_convert_fusion.1 = bf16[128,8192]{1,0:T(8,128)(2,1)} fusion(bf16[1,512,8192]{2,1,0:T(8,128)(2,1)} %param.29, bf16[128,8192]{1,0:T(8,128)(2,1)S(1)} %copy-done.1, bf16[1,8192,512]{2,1,0:T(8,128)(2,1)} %param.28, f32[128,512]{1,0:T(8,128)S(1)} %fusion.16), kind=kOutput, calls=%fused_computation.21 | convolution fusion | flops 2148925440 | bytes 21233664 | tf_op jit(solution)/shard_map/dot_general | solution.py:132
  513.6 66.4 %reduce-scatter.3.cloned.1.call-done = bf16[16,8192]{1,0:T(8,128)(2,1)} async-done(((bf16[128,8192]{1,0:T(8,128)(2,1)}), bf16[16,8192]{1,0:T(8,128)(2,1)}) %reduce-scatter.3.cloned.1.call-update) | async-done | bytes 262160 | tf_op jit(solution)/shard_map/reduce_scatter | solution.py:131
  580.1 6.6 convolution_convert_fusion
  586.7 70.4 %reduce-scatter.5.cloned.1.call-done = bf16[512,2048]{1,0:T(8,128)(2,1)} async-done(((bf16[512,8192]{1,0:T(8,128)(2,1)}), bf16[512,2048]{1,0:T(8,128)(2,1)}) %reduce-scatter.5.cloned.1.call-update) | async-done | bytes 2097168 | tf_op jit(solution)/shard_map/reduce_scatter | solution.py:145
  657.1 3.7 fusion.21
  (115 shorter events, 35.3 us)
Async XLA Ops:
  6.5 506.9 %copy-start = (bf16[8192,1]{0,1:T(2,128)(2,1)S(1)}, bf16[8192,1]{0,1:T(2,128)(2,1)}, u32[]{:S(2)}) copy-start(bf16[8192,1]{0,1:T(2,128)(2,1)} %param.26) | copy-start | bytes 49156
  6.5 130.1 %all-gather.5.cloned.1.call-start = ((), (), s32[]{:S(2)}) async-start(), calls=%async_computation.3 | async-start | bytes 9437184 | tf_op jit(solution)/shard_map/all_gather | solution.py:83
  7.3 254.2 %all-gather.7.cloned.1.call-start = ((), (), s32[]{:S(2)}) async-start(), calls=%async_computation.4 | async-start | bytes 9437184 | tf_op jit(solution)/shard_map/all_gather | solution.py:84
  8.0 405.8 %all-gather.9.cloned.1.call-start = ((), (), s32[]{:S(2)}) async-start(), calls=%async_computation.5 | async-start | bytes 5242880 | tf_op jit(solution)/shard_map/all_gather | solution.py:104
  328.5 4.9 copy-start.6
  328.5 5.7 copy-start.7
  328.5 5.7 copy-start.5
  333.2 164.8 %all-gather.11.cloned.1.call-start = ((), (), s32[]{:S(2)}) async-start(), calls=%async_computation.6 | async-start | bytes 2359296 | tf_op jit(solution)/shard_map/all_gather | solution.py:127
  428.0 20.8 %copy-start.2 = (bf16[512,2048]{1,0:T(8,128)(2,1)}, bf16[512,2048]{1,0:T(8,128)(2,1)S(1)}, u32[]{:S(2)}) copy-start(bf16[512,2048]{1,0:T(8,128)(2,1)S(1)} %get-tuple-element.425) | copy-start | bytes 6291460
  448.8 131.3 %reduce-scatter.3.cloned.1.call-start = ((), (), s32[]{:S(2)}) async-start(), calls=%async_computation.7 | async-start | bytes 2359296 | tf_op jit(solution)/shard_map/reduce_scatter | solution.py:131
  498.0 5.4 copy-start.1
  503.5 10.0 %copy-start.4 = (bf16[4,2,8,2048]{3,2,0,1:T(8,128)(2,1)S(1)}, bf16[4,2,8,2048]{3,2,0,1:T(8,128)(2,1)}, u32[]{:S(2)}) copy-start(bf16[4,2,8,2048]{3,2,0,1:T(8,128)(2,1)} %copy.67) | copy-start | bytes 786436
  513.1 144.0 %reduce-scatter.5.cloned.1.call-start = ((), (), s32[]{:S(2)}) async-start(), calls=%async_computation.8 | async-start | bytes 10485760 | tf_op jit(solution)/shard_map/reduce_scatter | solution.py:145
  586.6 70.5 %copy-start.3 = (bf16[512,2048]{1,0:T(8,128)(2,1)S(1)}, bf16[512,2048]{1,0:T(8,128)(2,1)}, u32[]{:S(2)}) copy-start(bf16[512,2048]{1,0:T(8,128)(2,1)} %copy-done.2) | copy-start | bytes 6291460
Sparse Core Ops, SparseCore 0:
  9.5 127.1 all-gather.4
  138.8 122.6 all-gather.6
  333.3 80.4 all-gather.8
  448.9 49.0 all-gather.10
  513.2 66.7 reduce-scatter.2
  586.8 70.2 reduce-scatter.4
where the time goes:
time: 669 us; the launch traced here: 668 us
  waiting for transfers between devices  506 us (76%)
  local copies, waits for them, and re-layouts  59.3 us (9%)
  matrix products  41 us (6%)
  loops' own time  20.9 us (3%)
  blocking collectives  14.6 us (2%)
  between operations  13.7 us (2%)
  other arithmetic  11.6 us (2%)
    all_gather x1, waiting for transfers between devices, shards(): key_piece = lax.all_gather(keys, 'seq', axis=0, tiled=True)  126 us
    all_gather x1, waiting for transfers between devices, shards(): value_piece = lax.all_gather(values, 'seq', axis=0, tiled=True)  113 us
    all_gather x1, waiting for transfers between devices, shards(): lax.all_gather(attended, 'exp', axis=1, tiled=True)  79.5 us
    reduce_scatter x1, waiting for transfers between devices, shards(): lax.psum_scatter(spread.astype(jnp.bfloat16), 'exp', scatter_dimension=1,...  70.4 us
    reduce_scatter x1, waiting for transfers between devices, shards(): lax.psum_scatter(jnp.dot(inner_act, w_down[0], preferred_element_type=jnp...  66.4 us
    all_gather x1, waiting for transfers between devices, shards(): piece = lax.all_gather(expert_rows, 'seq', axis=0, tiled=True)  49.2 us
    while x4, local copies, waits for them, and re-layouts, shards(): lax.scan(scan_step, state, (jnp.arange(blocks, dtype=jnp.int32), key_stac...  25.5 us
    another operation x1, loops' own time, shards(): lax.scan(scan_step, state, (jnp.arange(blocks, dtype=jnp.int32), key_stac...  20.7 us
  transfers between devices with their start and end apart: 6, of which 6 were waited for; matrix products, arithmetic and copies ran while one was open for 2% of the time, Pallas kernels for 0%

commit v1 on v0

--- a/solution.py
+++ b/solution.py
@@ -7,6 +7,18 @@
 D = 8192
 HD = 128
 block_rows = 512
+
+
+def detail_the_task(axis_tag, local_array, pos_dim):
+    axis_total = lax.axis_size(axis_tag)
+    found = [(c, (c + 1) % axis_total) for c in range(axis_total)]
+    finding = [None] * axis_total
+    finding[axis_total - 1] = local_array
+    for b in range(axis_total - 2, -1, -1):
+        finding[b] = lax.ppermute(finding[b + 1], axis_tag, found)
+    front = jnp.concatenate(finding, axis=pos_dim)
+    b_next = (lax.axis_index(axis_tag) + 1) * local_array.shape[pos_dim]
+    return jnp.roll(front, b_next, axis=pos_dim)
 
 
 def shards(
@@ -80,7 +92,7 @@
         jnp.zeros((tokens, heads_here, HD), jnp.float32),
     )
     state = initial
-    key_piece = lax.all_gather(keys, "seq", axis=0, tiled=True)
+    key_piece = detail_the_task("seq", keys, 0)
     value_piece = lax.all_gather(values, "seq", axis=0, tiled=True)
     row_count = key_piece.shape[0]
     blocks = row_count // block_rows

time: 669 us -> 734 us (1.097)
  local copies, waits for them, and re-layouts: 59.3 us -> 96.5 us
  waiting for transfers between devices: 506 us -> 531 us
    ppermute x0 -> x7, waiting for transfers between devices: none -> 267 us  [detail_the_task(): finding[b] = lax.ppermute(finding[b + 1], axis_tag, found)]
    all_gather x1 -> x0, waiting for transfers between devices: 126 us -> none  [shards(): key_piece = lax.all_gather(keys, 'seq', axis=0, tiled=True)]
    all_gather x1, waiting for transfers between devices: 113 us -> 0.01 us  [shards(): value_piece = lax.all_gather(values, 'seq', axis=0, tiled=True)]
    unnamed x17 -> x50, local copies, waits for them, and re-layouts: 1.54 us -> 29.9 us
    dynamic_slice x0 -> x1, local copies, waits for them, and re-layouts: none -> 7.59 us  [detail_the_task(): return jnp.roll(front, b_next, axis=pos_dim)]
  transfers between devices with their start and end apart: 6 -> 12, of which waited for: 6 -> 11; matrix products, arithmetic and copies ran while one was open for 2% -> 7% of each run, Pallas kernels for 0% -> 0%
where the time goes in v1:
time: 734 us; the launch traced here: 732 us
  waiting for transfers between devices  531 us (72%)
  local copies, waits for them, and re-layouts  96.5 us (13%)
  matrix products  41 us (6%)
  loops' own time  20.6 us (3%)
  blocking collectives  14.6 us (2%)
  between operations  13.4 us (2%)
  other arithmetic  11.6 us (2%)
    ppermute x7, waiting for transfers between devices, detail_the_task(): finding[b] = lax.ppermute(finding[b + 1], axis_tag, found)  267 us
    all_gather x1, waiting for transfers between devices, shards(): lax.all_gather(attended, 'exp', axis=1, tiled=True)  77.2 us
    reduce_scatter x1, waiting for transfers between devices, shards(): lax.psum_scatter(spread.astype(jnp.bfloat16), 'exp', scatter_dimension=1,...  70.5 us
    reduce_scatter x1, waiting for transfers between devices, shards(): lax.psum_scatter(jnp.dot(inner_act, w_down[0], preferred_element_type=jnp...  66.5 us
    all_gather x1, waiting for transfers between devices, shards(): piece = lax.all_gather(expert_rows, 'seq', axis=0, tiled=True)  49.2 us
    unnamed x50, local copies, waits for them, and re-layouts  29.9 us
    while x4, local copies, waits for them, and re-layouts, shards(): lax.scan(scan_step, state, (jnp.arange(blocks, dtype=jnp.int32), key_stac...  26.3 us
    another operation x1, loops' own time, shards(): lax.scan(scan_step, state, (jnp.arange(blocks, dtype=jnp.int32), key_stac...  20.4 us
  transfers between devices with their start and end apart: 12, of which 11 were waited for; matrix products, arithmetic and copies ran while one was open for 7% of the time, Pallas kernels for 0%

profile of v1, /device:TPU:0, one launch (start us, length us, event | category | flops | bytes accessed | tf_op | source)
XLA Modules:
  0.0 732.3 jit_solution(835996140098449053)
XLA Ops:
  10.3 37.5 %collective-permute-done = bf16[512,1024]{1,0:T(8,128)(2,1)S(1)} collective-permute-done((bf16[512,1024]{1,0:T(8,128)(2,1)}, bf16[512,1024]{1,0:T(8,128)(2,1)S(1)}, u32[]{:S(2)}, u32[]{:S(2)}) %collective-permute-start) | collective-permute-done | bytes 1048608 | tf_op jit(solution)/shard_map/ppermute | solution.py:18
  47.8 45.2 %collective-permute-done.1 = bf16[512,1024]{1,0:T(8,128)(2,1)S(1)} collective-permute-done((bf16[512,1024]{1,0:T(8,128)(2,1)S(1)}, bf16[512,1024]{1,0:T(8,128)(2,1)S(1)}, u32[]{:S(2)}, u32[]{:S(2)}) %collective-permute-start.1) | collective-permute-done | bytes 1048608 | tf_op jit(solution)/shard_map/ppermute | solution.py:18
  94.0 50.5 %collective-permute-done.2 = bf16[512,1024]{1,0:T(8,128)(2,1)S(1)} collective-permute-done((bf16[512,1024]{1,0:T(8,128)(2,1)S(1)}, bf16[512,1024]{1,0:T(8,128)(2,1)S(1)}, u32[]{:S(2)}, u32[]{:S(2)}) %collective-permute-start.2) | collective-permute-done | bytes 1048608 | tf_op jit(solution)/shard_map/ppermute | solution.py:18
  145.5 50.3 %collective-permute-done.3 = bf16[512,1024]{1,0:T(8,128)(2,1)S(1)} collective-permute-done((bf16[512,1024]{1,0:T(8,128)(2,1)S(1)}, bf16[512,1024]{1,0:T(8,128)(2,1)S(1)}, u32[]{:S(2)}, u32[]{:S(2)}) %collective-permute-start.3) | collective-permute-done | bytes 1048608 | tf_op jit(solution)/shard_map/ppermute | solution.py:18
  196.9 35.2 %collective-permute-done.4 = bf16[512,1024]{1,0:T(8,128)(2,1)S(1)} collective-permute-done((bf16[512,1024]{1,0:T(8,128)(2,1)S(1)}, bf16[512,1024]{1,0:T(8,128)(2,1)S(1)}, u32[]{:S(2)}, u32[]{:S(2)}) %collective-permute-start.4) | collective-permute-done | bytes 1048608 | tf_op jit(solution)/shard_map/ppermute | solution.py:18
  233.1 26.8 %collective-permute-done.5 = bf16[512,1024]{1,0:T(8,128)(2,1)} collective-permute-done((bf16[512,1024]{1,0:T(8,128)(2,1)S(1)}, bf16[512,1024]{1,0:T(8,128)(2,1)}, u32[]{:S(2)}, u32[]{:S(2)}) %collective-permute-start.5) | collective-permute-done | bytes 1048608 | tf_op jit(solution)/shard_map/ppermute | solution.py:18
  264.9 21.3 %collective-permute-done.6 = bf16[512,1024]{1,0:T(8,128)(2,1)} collective-permute-done((bf16[512,1024]{1,0:T(8,128)(2,1)}, bf16[512,1024]{1,0:T(8,128)(2,1)}, u32[]{:S(2)}, u32[]{:S(2)}) %collective-permute-start.6) | collective-permute-done | bytes 1048608 | tf_op jit(solution)/shard_map/ppermute | solution.py:18
  310.7 7.6 %constant_dynamic-slice_fusion.3 = bf16[4096,1024]{1,0:T(8,128)(2,1)} fusion(bf16[8192,1024]{1,0:T(8,128)(2,1)} %constant_dynamic-update-slice_fusion, s32[]{:T(128)S(6)} %select_n.66), kind=kLoop, calls=%fused_computation.88 | loop fusion | bytes 16777220 | tf_op jit(solution)/shard_map/jit(_roll_dynamic)/dynamic_slice | solution.py:21
  318.3 11.4 %copy.57 = bf16[8,512,1024]{1,2,0:T(8,128)(2,1)} copy(bf16[8,512,1024]{2,1,0:T(8,128)(2,1)} %bitcast.76) | data formatting | bytes 16777216 | tf_op jit(solution)/shard_map/while | solution.py:106
  329.7 11.4 %copy.59 = bf16[8,512,1024]{1,2,0:T(8,128)(2,1)} copy(bf16[8,512,1024]{2,1,0:T(8,128)(2,1)} %bitcast.78) | data formatting | bytes 16777216 | tf_op jit(solution)/shard_map/while | solution.py:106
  341.3 54.4 %while.18 = (s32[]{:T(128)}, f32[512,8]{0,1:T(8,128)S(1)}, f32[512,8]{0,1:T(8,128)S(1)}, f32[512,8,128]{2,0,1:T(8,128)S(1)}, s32[8]{0:T(128)S(1)}, /*index=5*/s3...) while((s32[]{:T(128)}, f32[512,8]{0,1:T(8,128)S(1)}, ...), condition=%wide.region_5.6_spmd, body=%wide.region_0.5_spmd.sunk | while | flops 1098654208 | bytes 38025672 | solution.py:106
  346.8 9.6 %conditional.2 = (f32[512,8]{0,1:T(8,128)S(1)}, f32[512,8]{0,1:T(8,128)S(1)}, f32[512,8,128]{2,0,1:T(8,128)S(1)}) conditional(s32[]{:T(128)} %convert_element_type.103, (s32[]{:T(128)}, s32[512]{0:T(512)S(1)}, s32[4096]{0:T(1024)}, s32[512]{0:T(512)S(1)}, bf16[8,512,1024]{1,2,0:T(8,128)(2,1)}, /*index=5*/s32[]{:T(128)}, ...), branch_computations={%region_1.3_spmd, %region_4.4_spmd} | conditional | flops 1098654208 | bytes 37992520 | solution.py:82
  353.0 3.4 bitcast_add_fusion
  401.5 77.2 %all-gather.6.cloned.1.call-done = bf16[512,4096]{0,1:T(8,128)(2,1)} async-done(((bf16[512,1024]{0,1:T(8,128)(2,1)}), bf16[512,4096]{0,1:T(8,128)(2,1)}) %all-gather.6.cloned.1.call-update) | async-done | bytes 4194320 | tf_op jit(solution)/shard_map/all_gather | solution.py:116
  478.7 14.2 %fusion.18 = (f32[512]{0:T(512)S(1)}, bf16[512,2048]{1,0:T(8,128)(2,1)S(1)}) fusion(bf16[512,4096]{0,1:T(8,128)(2,1)} %all-gather.6.cloned.1.call-done, bf16[4096,2048]{1,0:T(8,128)(2,1)} %param.22, bf16[512,2048]{1,0:T(8,128)(2,1)} %param.17), kind=kOutput, calls=%fused_computation.30 | convolution fusion | flops 8596226048 | bytes 25167872 | tf_op jit(solution)/shard_map/dot_general | solution.py:115
  492.8 5.9 psum.7
  504.2 8.7 %all_to_all.5 = bf16[16,4,2048]{2,0,1:T(8,128)(2,1)S(1)} all-to-all(bf16[16,4,2048]{2,0,1:T(8,128)(2,1)S(1)} %fusion.34), channel_id=1, replica_groups=mesh['seq'=8,'exp'=4] {'exp'}, dimensions={1} | all-to-all | bytes 524288 | tf_op jit(solution)/shard_map/all_to_all | solution.py:136
  513.7 49.2 %all-gather.8.cloned.1.call-done = bf16[128,8192]{1,0:T(8,128)(2,1)} async-done(((bf16[16,8192]{1,0:T(8,128)(2,1)}), bf16[128,8192]{1,0:T(8,128)(2,1)}) %all-gather.8.cloned.1.call-update) | async-done | bytes 2097168 | tf_op jit(solution)/shard_map/all_gather | solution.py:139
  562.9 5.4 fusion.16
  568.3 9.6 %convolution_convert_fusion.1 = bf16[128,8192]{1,0:T(8,128)(2,1)} fusion(bf16[1,512,8192]{2,1,0:T(8,128)(2,1)} %param.29, bf16[128,8192]{1,0:T(8,128)(2,1)S(1)} %copy-done.1, bf16[1,8192,512]{2,1,0:T(8,128)(2,1)} %param.28, f32[128,512]{1,0:T(8,128)S(1)} %fusion.16), kind=kOutput, calls=%fused_computation.21 | convolution fusion | flops 2148925440 | bytes 21233664 | tf_op jit(solution)/shard_map/dot_general | solution.py:144
  578.5 66.5 %reduce-scatter.3.cloned.1.call-done = bf16[16,8192]{1,0:T(8,128)(2,1)} async-done(((bf16[128,8192]{1,0:T(8,128)(2,1)}), bf16[16,8192]{1,0:T(8,128)(2,1)}) %reduce-scatter.3.cloned.1.call-update) | async-done | bytes 262160 | tf_op jit(solution)/shard_map/reduce_scatter | solution.py:143
  645.0 6.6 convolution_convert_fusion
  651.6 70.5 %reduce-scatter.5.cloned.1.call-done = bf16[512,2048]{1,0:T(8,128)(2,1)} async-done(((bf16[512,8192]{1,0:T(8,128)(2,1)}), bf16[512,2048]{1,0:T(8,128)(2,1)}) %reduce-scatter.5.cloned.1.call-update) | async-done | bytes 2097168 | tf_op jit(solution)/shard_map/reduce_scatter | solution.py:157
  722.1 3.7 fusion.21
  (161 shorter events, 80.5 us)
Async XLA Ops:
  6.5 571.7 %copy-start = (bf16[8192,1]{0,1:T(2,128)(2,1)S(1)}, bf16[8192,1]{0,1:T(2,128)(2,1)}, u32[]{:S(2)}) copy-start(bf16[8192,1]{0,1:T(2,128)(2,1)} %param.26) | copy-start | bytes 49156
  6.5 323.1 %all-gather.4.cloned.1.call-start = ((), (), s32[]{:S(2)}) async-start(), calls=%async_computation.3 | async-start | bytes 9437184 | tf_op jit(solution)/shard_map/all_gather | solution.py:96
  7.3 471.4 %all-gather.6.cloned.1.call-start = ((), (), s32[]{:S(2)}) async-start(), calls=%async_computation.4 | async-start | bytes 5242880 | tf_op jit(solution)/shard_map/all_gather | solution.py:116
  7.3 40.5 %collective-permute-start = (bf16[512,1024]{1,0:T(8,128)(2,1)}, bf16[512,1024]{1,0:T(8,128)(2,1)S(1)}, u32[]{:S(2)}, u32[]{:S(2)}) collective-permute-start(bf16[512,1024]{1,0:T(8,128)(2,1)} %param.19), channel_id=1, source_target_pairs={{0,4},{4,8},{8,12},{12,16},{16,20},{20,24},{24,28},{28,0},{1,5},{5... | collective-permute-start | bytes 3145736 | tf_op jit(solution)/shard_map/ppermute | solution.py:18
  47.8 45.2 %collective-permute-start.1 = (bf16[512,1024]{1,0:T(8,128)(2,1)S(1)}, bf16[512,1024]{1,0:T(8,128)(2,1)S(1)}, u32[]{:S(2)}, u32[]{:S(2)}) collective-permute-start(bf16[512,1024]{1,0:T(8,128)(2,1)S(1)} %collective-permute-done), channel_id=1, source_target_pairs={{0,4},{4,8},{8,12},{12,16},{16,20},{20,24},{24,28},{28,0},{1,5},{5... | collective-permute-start | bytes 3145736 | tf_op jit(solution)/shard_map/ppermute | solution.py:18
  94.0 50.5 %collective-permute-start.2 = (bf16[512,1024]{1,0:T(8,128)(2,1)S(1)}, bf16[512,1024]{1,0:T(8,128)(2,1)S(1)}, u32[]{:S(2)}, u32[]{:S(2)}) collective-permute-start(bf16[512,1024]{1,0:T(8,128)(2,1)S(1)} %collective-permute-done.1), channel_id=1, source_target_pairs={{0,4},{4,8},{8,12},{12,16},{16,20},{20,24},{24,28},{28,0},{1,5},{5... | collective-permute-start | bytes 3145736 | tf_op jit(solution)/shard_map/ppermute | solution.py:18
  145.5 50.3 %collective-permute-start.3 = (bf16[512,1024]{1,0:T(8,128)(2,1)S(1)}, bf16[512,1024]{1,0:T(8,128)(2,1)S(1)}, u32[]{:S(2)}, u32[]{:S(2)}) collective-permute-start(bf16[512,1024]{1,0:T(8,128)(2,1)S(1)} %collective-permute-done.2), channel_id=1, source_target_pairs={{0,4},{4,8},{8,12},{12,16},{16,20},{20,24},{24,28},{28,0},{1,5},{5... | collective-permute-start | bytes 3145736 | tf_op jit(solution)/shard_map/ppermute | solution.py:18
  196.9 35.2 %collective-permute-start.4 = (bf16[512,1024]{1,0:T(8,128)(2,1)S(1)}, bf16[512,1024]{1,0:T(8,128)(2,1)S(1)}, u32[]{:S(2)}, u32[]{:S(2)}) collective-permute-start(bf16[512,1024]{1,0:T(8,128)(2,1)S(1)} %collective-permute-done.3), channel_id=1, source_target_pairs={{0,4},{4,8},{8,12},{12,16},{16,20},{20,24},{24,28},{28,0},{1,5},{5... | collective-permute-start | bytes 3145736 | tf_op jit(solution)/shard_map/ppermute | solution.py:18
  233.1 26.8 %collective-permute-start.5 = (bf16[512,1024]{1,0:T(8,128)(2,1)S(1)}, bf16[512,1024]{1,0:T(8,128)(2,1)}, u32[]{:S(2)}, u32[]{:S(2)}) collective-permute-start(bf16[512,1024]{1,0:T(8,128)(2,1)S(1)} %collective-permute-done.4), channel_id=1, source_target_pairs={{0,4},{4,8},{8,12},{12,16},{16,20},{20,24},{24,28},{28,0},{1,5},{5... | collective-permute-start | bytes 3145736 | tf_op jit(solution)/shard_map/ppermute | solution.py:18
  259.9 26.2 %collective-permute-start.6 = (bf16[512,1024]{1,0:T(8,128)(2,1)}, bf16[512,1024]{1,0:T(8,128)(2,1)}, u32[]{:S(2)}, u32[]{:S(2)}) collective-permute-start(bf16[512,1024]{1,0:T(8,128)(2,1)} %collective-permute-done.5), channel_id=1, source_target_pairs={{0,4},{4,8},{8,12},{12,16},{16,20},{20,24},{24,28},{28,0},{1,5},{5... | collective-permute-start | bytes 3145736 | tf_op jit(solution)/shard_map/ppermute | solution.py:18
  262.2 36.3 %copy-start.4 = (bf16[512,1024]{1,0:T(8,128)(2,1)S(1)}, bf16[512,1024]{1,0:T(8,128)(2,1)}, u32[]{:S(2)}) copy-start(bf16[512,1024]{1,0:T(8,128)(2,1)} %param.19) | copy-start | bytes 3145732
  263.9 31.5 %copy-start.8 = (bf16[512,1024]{1,0:T(8,128)(2,1)S(1)}, bf16[512,1024]{1,0:T(8,128)(2,1)}, u32[]{:S(2)}) copy-start(bf16[512,1024]{1,0:T(8,128)(2,1)} %copy-done.7) | copy-start | bytes 3145732
  263.9 32.5 %copy-start.6 = (bf16[512,1024]{1,0:T(8,128)(2,1)S(1)}, bf16[512,1024]{1,0:T(8,128)(2,1)}, u32[]{:S(2)}) copy-start(bf16[512,1024]{1,0:T(8,128)(2,1)} %copy-done.5) | copy-start | bytes 3145732
  290.7 13.6 %copy-start.12 = (bf16[512,1024]{1,0:T(8,128)(2,1)S(1)}, bf16[512,1024]{1,0:T(8,128)(2,1)}, u32[]{:S(2)}) copy-start(bf16[512,1024]{1,0:T(8,128)(2,1)} %copy-done.11) | copy-start | bytes 3145732
  293.0 12.3 %copy-start.10 = (bf16[512,1024]{1,0:T(8,128)(2,1)S(1)}, bf16[512,1024]{1,0:T(8,128)(2,1)}, u32[]{:S(2)}) copy-start(bf16[512,1024]{1,0:T(8,128)(2,1)} %copy-done.9) | copy-start | bytes 3145732
  395.7 5.7 copy-start.16
  395.7 5.8 copy-start.14
  400.4 162.4 %all-gather.8.cloned.1.call-start = ((), (), s32[]{:S(2)}) async-start(), calls=%async_computation.5 | async-start | bytes 2359296 | tf_op jit(solution)/shard_map/all_gather | solution.py:139
  492.8 20.8 %copy-start.2 = (bf16[512,2048]{1,0:T(8,128)(2,1)}, bf16[512,2048]{1,0:T(8,128)(2,1)S(1)}, u32[]{:S(2)}) copy-start(bf16[512,2048]{1,0:T(8,128)(2,1)S(1)} %get-tuple-element.425) | copy-start | bytes 6291460
  513.6 131.4 %reduce-scatter.3.cloned.1.call-start = ((), (), s32[]{:S(2)}) async-start(), calls=%async_computation.6 | async-start | bytes 2359296 | tf_op jit(solution)/shard_map/reduce_scatter | solution.py:143
  562.9 5.4 copy-start.1
  568.3 10.0 %copy-start.13 = (bf16[4,2,8,2048]{3,2,0,1:T(8,128)(2,1)S(1)}, bf16[4,2,8,2048]{3,2,0,1:T(8,128)(2,1)}, u32[]{:S(2)}) copy-start(bf16[4,2,8,2048]{3,2,0,1:T(8,128)(2,1)} %copy.67) | copy-start | bytes 786436
  577.9 144.1 %reduce-scatter.5.cloned.1.call-start = ((), (), s32[]{:S(2)}) async-start(), calls=%async_computation.7 | async-start | bytes 10485760 | tf_op jit(solution)/shard_map/reduce_scatter | solution.py:157
  578.5 143.6 %copy-start.3 = (bf16[512,2048]{1,0:T(8,128)(2,1)S(1)}, bf16[512,2048]{1,0:T(8,128)(2,1)}, u32[]{:S(2)}) copy-start(bf16[512,2048]{1,0:T(8,128)(2,1)} %copy-done.2) | copy-start | bytes 6291460
  (5 other events, 9.0 us)
Sparse Core Ops, SparseCore 0:
  9.5 190.4 all-gather.3
  400.5 78.0 all-gather.5
  513.7 49.0 all-gather.7
  578.1 66.8 reduce-scatter.2
  651.7 70.3 reduce-scatter.4
